TPU v7x, 32 devices: a whole 2x2x4 slice. The times are simulated.
32 devices in a mesh: frames: 8 (over z, y), band: 4 (over x, core).
Axes of the slice: x: 2, y: 2, z: 4, core: 2. Of those that a mesh axis runs over, the one named last changes fastest.
Arguments:
- tokens: bfloat16 [16, 1024, 1024], P('frames', 'band'), may hold values from -6 to 6
- norm_space: float32 [1024], replicated, may hold values from 0.5 to 1.5
- query_space: bfloat16 [1024, 1024], replicated, may hold values from -0.1875 to 0.1875
- keyval_space: bfloat16 [1024, 512], replicated, may hold values from -0.1875 to 0.1875
- out_space: bfloat16 [1024, 1024], replicated, may hold values from -0.1875 to 0.1875
- qk_space: float32 [2, 64], replicated, may hold values from 0.7 to 7
- norm_time: float32 [1024], replicated, may hold values from 0.5 to 1.5
- query_time: bfloat16 [1024, 1024], replicated, may hold values from -0.1875 to 0.1875
- keyval_time: bfloat16 [1024, 512], replicated, may hold values from -0.1875 to 0.1875
- out_time: bfloat16 [1024, 1024], replicated, may hold values from -0.1875 to 0.1875
- qk_time: float32 [2, 64], replicated, may hold values from 0.7 to 7
Outputs:
- mixed: bfloat16 [16, 1024, 1024], P('frames', 'band')
All inputs are finite; a program needn't handle non-finite values.
Results may differ from a plain program's by a relative error of at most 0.025.
The roundings to bfloat16 on the way count: a program that leaves them out, or rounds other values in their place, can miss the bound.
Values may be sent and summed in bfloat16 or wider, within the bound.
No kernel may reach another device: no remote copies, remote signals or barrier semaphores. Data moves between devices by JAX's collectives and lax.ppermute only.
A program may use at most 128 MiB of HBM per device.

v0:
```python
import jax
import jax.numpy as jnp
from jax import lax
from jax.sharding import PartitionSpec as P

HEADS = 16
KV_HEADS = 4
HEAD_DIM = 64


def rms_rows(values, gain):
    values = values.astype(jnp.float32)
    scaled = lax.rsqrt(jnp.mean(values * values, axis=-1, keepdims=True) + 1e-06)
    return values * scaled * gain


def project(hidden, w_query, w_keyval, qk_gain):
    row_count = hidden.shape[0]
    queries = jnp.dot(hidden, w_query, preferred_element_type=jnp.float32)
    keyval = jnp.dot(hidden, w_keyval, preferred_element_type=jnp.float32)
    queries = rms_rows(queries.reshape(row_count, HEADS, HEAD_DIM), qk_gain[0])
    key_part = keyval[:, : KV_HEADS * HEAD_DIM].reshape(row_count, KV_HEADS, HEAD_DIM)
    key_rows = rms_rows(key_part, qk_gain[1])
    values = keyval[:, KV_HEADS * HEAD_DIM :]
    return (
        queries.reshape(row_count, -1).astype(jnp.bfloat16),
        key_rows.reshape(row_count, -1).astype(jnp.bfloat16),
        values.astype(jnp.bfloat16),
    )


def attend(queries, key_rows, values, causal_mask):
    query_count = queries.shape[0]
    key_count = key_rows.shape[0]
    groups = HEADS // KV_HEADS
    grouped = queries.reshape(query_count, KV_HEADS, groups, HEAD_DIM)
    key_heads = key_rows.reshape(key_count, KV_HEADS, HEAD_DIM)
    value_heads = values.reshape(key_count, KV_HEADS, HEAD_DIM)
    scores = jnp.einsum(
        "nkgd,mkd->kgnm", grouped, key_heads, preferred_element_type=jnp.float32
    ) * HEAD_DIM ** (-0.5)
    if causal_mask is not None:
        scores = jnp.where(causal_mask, scores, -jnp.inf)
    largest = jnp.max(scores, axis=-1, keepdims=True)
    expos = jnp.exp(scores - largest)
    totals = jnp.sum(expos, axis=-1)
    weights = expos.astype(jnp.bfloat16)
    summed = jnp.einsum("kgnm,mkd->nkgd", weights, value_heads, preferred_element_type=jnp.float32)
    summed = summed / jnp.transpose(totals, (2, 0, 1))[..., None]
    return summed.reshape(query_count, HEADS * HEAD_DIM).astype(jnp.bfloat16)


def body(
    tokens,
    norm_space,
    query_space,
    keyval_space,
    out_space,
    qk_space,
    norm_time,
    query_time,
    keyval_time,
    out_time,
    qk_time,
):
    frames_here, rows_here, model_width = tokens.shape
    flat_tokens = tokens.reshape(frames_here * rows_here, model_width)
    normed = rms_rows(flat_tokens, norm_space).astype(jnp.bfloat16)
    queries, key_rows, values = project(normed, query_space, keyval_space, qk_space)
    queries = queries.reshape(frames_here, rows_here, -1)
    key_rows = key_rows.reshape(frames_here, rows_here, -1)
    values = values.reshape(frames_here, rows_here, -1)
    all_keys, all_values = (
        lax.all_gather(key_rows, "band", axis=1, tiled=True),
        lax.all_gather(values, "band", axis=1, tiled=True),
    )

    def space_frame(pieces):
        frame_q, frame_k, frame_v = pieces
        return attend(frame_q, frame_k, frame_v, None)

    attended = lax.map(space_frame, (queries, all_keys, all_values))
    attended = attended.reshape(frames_here * rows_here, HEADS * HEAD_DIM)
    update = jnp.dot(attended, out_space, preferred_element_type=jnp.float32)
    stream = (flat_tokens.astype(jnp.float32) + update).astype(jnp.bfloat16)
    normed_time = rms_rows(stream, norm_time).astype(jnp.bfloat16)
    moved = lax.all_to_all(
        normed_time.reshape(frames_here, rows_here, model_width),
        "frames",
        split_axis=1,
        concat_axis=0,
        tiled=True,
    )
    frame_total, local_positions = (moved.shape[0], moved.shape[1])
    time_q, time_k, time_v = project(
        moved.reshape(frame_total * local_positions, model_width), query_time, keyval_time, qk_time
    )
    time_q = time_q.reshape(frame_total, local_positions, -1)
    time_k = time_k.reshape(frame_total, local_positions, -1)
    time_v = time_v.reshape(frame_total, local_positions, -1)
    order = jnp.arange(frame_total, dtype=jnp.int32)
    causal_mask = order[:, None] >= order[None, :]
    time_att = jax.vmap(lambda qq, kk, vv: attend(qq, kk, vv, causal_mask))(
        jnp.swapaxes(time_q, 0, 1), jnp.swapaxes(time_k, 0, 1), jnp.swapaxes(time_v, 0, 1)
    )
    time_att = jnp.swapaxes(time_att, 0, 1)
    returned = lax.all_to_all(time_att, "frames", split_axis=0, concat_axis=1, tiled=True)
    returned = returned.reshape(frames_here * rows_here, HEADS * HEAD_DIM)
    update_time = jnp.dot(returned, out_time, preferred_element_type=jnp.float32)
    mixed = (stream.astype(jnp.float32) + update_time).astype(jnp.bfloat16)
    return mixed.reshape(frames_here, rows_here, model_width)


def solution(mesh):
    placed = (P("frames", "band", None), P(), P(), P(), P(), P(), P(), P(), P(), P(), P())
    return jax.shard_map(
        body, mesh=mesh, in_specs=placed, out_specs=P("frames", "band", None), check_vma=False
    )
```

profile of v0, /device:TPU:0, one launch (start us, length us, event | category | flops | bytes accessed | tf_op | source)
XLA Modules:
  0.0 223.1 jit_solution(13843182820674432862)
XLA Ops:
  16.3 4.0 %copy.70 = bf16[1024,1024]{0,1:T(8,128)(2,1)} copy(bf16[1024,1024]{1,0:T(8,128)(2,1)} %param.15) | data formatting | bytes 4194304 | tf_op args[2]
  24.8 2.4 %copy.71 = bf16[2,256,1024]{1,2,0:T(8,128)(2,1)} copy(bf16[2,256,1024]{1,0,2:T(2,128)(2,1)} %convert_element_type.87) | data formatting | bytes 2097152 | tf_op jit(solution)/shard_map/while | solution.py:82
  27.2 6.7 %all-gather.5.cloned.1.call-done = bf16[2,1024,256]{1,2,0:T(8,128)(2,1)} async-done(((bf16[2,256,256]{1,2,0:T(8,128)(2,1)}), bf16[2,1024,256]{1,2,0:T(8,128)(2,1)}) %all-gather.5.cloned.1.call-update) | async-done | bytes 1048592 | tf_op jit(solution)/shard_map/all_gather | solution.py:74
  33.9 18.4 %all-gather.3.cloned.1.call-done = bf16[2,1024,256]{1,2,0:T(8,128)(2,1)} async-done(((bf16[2,256,256]{1,2,0:T(8,128)(2,1)}), bf16[2,1024,256]{1,2,0:T(8,128)(2,1)}) %all-gather.3.cloned.1.call-update) | async-done | bytes 1048592 | tf_op jit(solution)/shard_map/all_gather | solution.py:75
  52.3 57.7 %while.10 = (s32[]{:T(128)}, bf16[2,256,1024]{2,1,0:T(8,128)(2,1)}, bf16[2,1024,256]{1,2,0:T(8,128)(2,1)}, bf16[2,1024,256]{1,2,0:T(8,128)(2,1)}, bf16[2,256,1024]{1,2,0:T(8,128)(2,1)}, /*index=5*/s32[]{:T(128)}) while((s32[]{:T(128)}, bf16[2,256,1024]{2,1,0:T(8,128)(2,1)}, bf16[2,1024,256]{1,2,0:T(8,128)(2,1)}, ...), condition=%wide.region_6.7_spmd, body=%wide.region_3.6_spmd.sunk | while | flops 1107812352 | bytes 57754188 | solution.py:82
  54.7 8.1 %bitcast_reduce_fusion.4 = (f32[4,4,256]{2,1,0:T(4,128)S(1)}, f32[4,1024,256,4]{2,1,3,0:T(8,128)}) fusion(bf16[1024,4,64,1]{0,2,3,1:T(8,128)(2,1)S(1)} %bitcast.152, bf16[256,4,4,64]{0,3,2,1:T(8,128)(2,1)S(1)} %bitcast.153), kind=kOutput, calls=%fused_computation.1.clone.1 | convolution fusion | flops 545255424 | bytes 17842176 | tf_op jit(solution)/shard_map/while/body/eval_jaxpr/nkgd,mkd->kgnm/dot_general | solution.py:39
  62.8 8.6 %fusion.63 = f32[4,4,256]{2,1,0:T(4,128)S(1)} fusion(f32[4,1024,256,4]{2,1,3,0:T(8,128)} %get-tuple-element.118, f32[4,4,256]{2,1,0:T(4,128)S(1)} %get-tuple-element.119), kind=kLoop, calls=%fused_computation.3.clone.1 | loop fusion | flops 12578816 | bytes 16809984 | tf_op jit(solution)/shard_map/while/body/eval_jaxpr/reduce_sum | solution.py:46
  71.4 8.7 %divide_convert_fusion.2 = bf16[256,4,4,64]{0,3,2,1:T(8,128)(2,1)S(1)} fusion(bf16[1024,4,64,1]{0,2,3,1:T(8,128)(2,1)S(1)} %bitcast.150, f32[4,1024,256,4]{2,1,3,0:T(8,128)} %get-tuple-element.118, f32[4,4,256]{2,1,0:T(4,128)S(1)} %get-tuple-element.119, f32[256,4,4]{0,2,1:T(4,128)S(1)} %bitcast.159), kind=kOutput, calls=%fused_computation.7.clone.1 | convolution fusion | flops 549978112 | bytes 17858560 | tf_op jit(solution)/shard_map/while/body/eval_jaxpr/kgnm,mkd->nkgd/dot_general | solution.py:48
  83.5 8.1 %bitcast_reduce_fusion.4 = (f32[4,4,256]{2,1,0:T(4,128)S(1)}, f32[4,1024,256,4]{2,1,3,0:T(8,128)}) fusion(bf16[1024,4,64,1]{0,2,3,1:T(8,128)(2,1)S(1)} %bitcast.152, bf16[256,4,4,64]{0,3,2,1:T(8,128)(2,1)S(1)} %bitcast.153), kind=kOutput, calls=%fused_computation.1.clone.1 | convolution fusion | flops 545255424 | bytes 17842176 | tf_op jit(solution)/shard_map/while/body/eval_jaxpr/nkgd,mkd->kgnm/dot_general | solution.py:39
  91.6 8.6 %fusion.63 = f32[4,4,256]{2,1,0:T(4,128)S(1)} fusion(f32[4,1024,256,4]{2,1,3,0:T(8,128)} %get-tuple-element.118, f32[4,4,256]{2,1,0:T(4,128)S(1)} %get-tuple-element.119), kind=kLoop, calls=%fused_computation.3.clone.1 | loop fusion | flops 12578816 | bytes 16809984 | tf_op jit(solution)/shard_map/while/body/eval_jaxpr/reduce_sum | solution.py:46
  100.2 8.7 %divide_convert_fusion.2 = bf16[256,4,4,64]{0,3,2,1:T(8,128)(2,1)S(1)} fusion(bf16[1024,4,64,1]{0,2,3,1:T(8,128)(2,1)S(1)} %bitcast.150, f32[4,1024,256,4]{2,1,3,0:T(8,128)} %get-tuple-element.118, f32[4,4,256]{2,1,0:T(4,128)S(1)} %get-tuple-element.119, f32[256,4,4]{0,2,1:T(4,128)S(1)} %bitcast.159), kind=kOutput, calls=%fused_computation.7.clone.1 | convolution fusion | flops 549978112 | bytes 17858560 | tf_op jit(solution)/shard_map/while/body/eval_jaxpr/kgnm,mkd->nkgd/dot_general | solution.py:48
  110.0 2.9 %fusion.15 = (f32[512]{0:T(512)S(1)}, bf16[512,1024]{1,0:T(8,128)(2,1)S(1)}) fusion(bf16[512,1024]{1,0:T(8,128)(2,1)} %bitcast.178, bf16[1024,1024]{1,0:T(8,128)(2,1)S(1)} %copy-done, bf16[2,256,1024]{2,1,0:T(8,128)(2,1)} %param.13), kind=kOutput, calls=%fused_computation.23 | convolution fusion | flops 1076887040 | bytes 5244928 | tf_op jit(solution)/shard_map/dot_general | solution.py:84
  116.3 5.5 %all-to-all-start = ((bf16[2,256,1024]{2,0,1:T(2,128)(2,1)}), bf16[2,256,1024]{2,0,1:T(2,128)(2,1)S(1)}, u32[]{:S(2)}, u32[]{:S(2)}) async-start(bf16[2,256,1024]{2,0,1:T(2,128)(2,1)} %copy.73), calls=%async_computation | async-start | bytes 2097152 | tf_op jit(solution)/shard_map/all_to_all | solution.py:87
  121.9 3.9 %copy.79 = bf16[1024,1024]{0,1:T(8,128)(2,1)} copy(bf16[1024,1024]{1,0:T(8,128)(2,1)} %param.20) | data formatting | bytes 4194304 | tf_op args[7]
  125.9 22.1 %all-to-all-done = bf16[2,256,1024]{2,0,1:T(2,128)(2,1)S(1)} async-done(((bf16[2,256,1024]{2,0,1:T(2,128)(2,1)}), bf16[2,256,1024]{2,0,1:T(2,128)(2,1)S(1)}, u32[]{:S(2)}, u32[]{:S(2)}) %all-to-all-start) | async-done | bytes 1048608 | tf_op jit(solution)/shard_map/all_to_all | solution.py:87
  153.8 3.2 %multiply_reduce_fusion = (f32[512,16]{0,1:T(8,128)S(1)}, f32[512,16,64]{0,2,1:T(8,128)S(1)}) fusion(bf16[512,1024,1]{1,0,2:T(8,128)(2,1)} %bitcast.169, bf16[16,64,1024]{2,1,0:T(8,128)(2,1)} %bitcast.160), kind=kOutput, calls=%fused_computation.43 | convolution fusion | flops 1074782208 | bytes 5275648 | tf_op jit(solution)/shard_map/dot_general | solution.py:19
  157.6 2.9 %copy.80 = bf16[512,16,64]{2,1,0:T(8,128)(2,1)} copy(bf16[512,16,64]{0,2,1:T(8,128)(2,1)S(1)} %multiply_convert_fusion) | data formatting | bytes 2097152 | tf_op jit(solution)/shard_map/convert_element_type | solution.py:26
  160.4 3.2 %convert_element_type.93 = bf16[16,32,1024]{2,1,0:T(8,128)(2,1)S(1)} reshape(bf16[512,16,64]{2,1,0:T(8,128)(2,1)} %copy.80) | data formatting | bytes 2097152 | tf_op jit(solution)/shard_map/convert_element_type | solution.py:26
  163.7 2.4 %reshape.186 = bf16[32,16,4,4,64]{4,3,2,0,1:T(4,128)(2,1)} reshape(bf16[32,16,1024]{2,0,1:T(8,128)(2,1)S(1)} %bitcast.154) | data formatting | bytes 2097152 | tf_op jit(solution)/shard_map/vmap()/reshape | solution.py:36
  166.4 6.9 %fusion.14 = (f32[32,4,4,16]{3,2,1,0:T(4,128)S(1)}, f32[32,4,16,16,4]{3,2,4,1,0:T(8,128)S(1)}) fusion(pred[16,16]{0,1:T(8,128)(4,1)S(1)} %iota_compare_fusion, bf16[32,16,4,4,64]{4,3,2,0,1:T(4,128)(2,1)} %reshape.186, bf16[32,16,4,64,1]{3,2,1,0,4:T(4,128)(2,1)} %bitcast.164), kind=kOutput, calls=%fused_computation.19 | convolution fusion | flops 17162240 | bytes 1868032 | tf_op jit(solution)/shard_map/vmap(nkgd,mkd->kgnm)/dot_general | solution.py:39
  175.0 2.4 %fusion.11 = bf16[32,16,4,4,64]{4,1,3,2,0:T(8,128)(2,1)S(1)} fusion(f32[32,4,16,16,4]{3,2,4,1,0:T(8,128)S(1)} %get-tuple-element.80, f32[32,16,4,4]{1,3,2,0:T(4,128)S(1)} %bitcast.176, f32[32,4,4,16]{3,2,1,0:T(4,128)S(1)} %get-tuple-element.79, pred[16,16]{0,1:T(8,128)(4,1)S(1)} %iota_compare_fusion, bf16[32,16,4,64,1]{3,2,1,0,4:T(4,128)(2,1)S(1)} %bitcast.175), kind=kOutput, calls=%fused_computation.14 | convolution fusion | flops 18350080 | bytes 1900800 | tf_op jit(solution)/shard_map/vmap(kgnm,mkd->nkgd)/dot_general | solution.py:48
  177.4 2.5 %copy.86 = bf16[32,16,4,4,64]{4,3,2,1,0:T(4,128)(2,1)} copy(bf16[32,16,4,4,64]{4,1,3,2,0:T(8,128)(2,1)S(1)} %fusion.11) | data formatting | bytes 2097152 | tf_op jit(solution)/shard_map/vmap()/convert_element_type | solution.py:50
  179.8 3.8 %convert_element_type.96 = bf16[32,16,1024]{2,1,0:T(8,128)(2,1)S(1)} reshape(bf16[32,16,4,4,64]{4,3,2,1,0:T(4,128)(2,1)} %copy.86) | data formatting | bytes 2097152 | tf_op jit(solution)/shard_map/vmap()/convert_element_type | solution.py:50
  184.3 29.6 %all_to_all.30 = bf16[16,32,1024]{2,1,0:T(8,128)(2,1)S(1)} all-to-all(bf16[16,32,1024]{2,1,0:T(8,128)(2,1)S(1)} %copy.87), channel_id=1, replica_groups=mesh['frames'=8,'band'=4] {'frames'}, dimensions={0} | all-to-all | bytes 2097152 | tf_op jit(solution)/shard_map/all_to_all | solution.py:107
  (93 shorter events, 35.5 us)
Async XLA Ops:
  6.5 103.5 %copy-start = (bf16[1024,1024]{1,0:T(8,128)(2,1)S(1)}, bf16[1024,1024]{1,0:T(8,128)(2,1)}, u32[]{:S(2)}) copy-start(bf16[1024,1024]{1,0:T(8,128)(2,1)} %param.17) | copy-start | bytes 6291460
  6.5 3.2 %copy-start.13 = (bf16[1024,512]{1,0:T(8,128)(2,1)S(1)}, bf16[1024,512]{1,0:T(8,128)(2,1)}, u32[]{:S(2)}) copy-start(bf16[1024,512]{1,0:T(8,128)(2,1)} %param.16) | copy-start | bytes 3145732
  6.5 27.4 %all-gather.5.cloned.1.call-start = ((), (), s32[]{:S(2)}) async-start(), calls=%async_computation.3 | async-start | bytes 1310720 | tf_op jit(solution)/shard_map/all_gather | solution.py:74
  10.5 1.0 copy-start.3
  11.5 0.7 copy-start.10
  14.2 38.1 %all-gather.3.cloned.1.call-start = ((), (), s32[]{:S(2)}) async-start(), calls=%async_computation.2 | async-start | bytes 1310720 | tf_op jit(solution)/shard_map/all_gather | solution.py:75
  16.2 4.0 %copy-start.1 = (bf16[2,256,1024]{2,1,0:T(8,128)(2,1)S(1)}, bf16[2,256,1024]{2,1,0:T(8,128)(2,1)}, u32[]{:S(2)}) copy-start(bf16[2,256,1024]{2,1,0:T(8,128)(2,1)} %param.13) | copy-start | bytes 3145732
  16.2 4.0 %copy-start.8 = (f32[1024]{0:T(1024)S(1)}, f32[1024]{0:T(1024)}, u32[]{:S(2)}) copy-start(f32[1024]{0:T(1024)} %param.14) | copy-start | bytes 12292
  20.3 1.6 copy-start.2
  110.0 3.9 %copy-start.9 = (f32[1024]{0:T(1024)S(1)}, f32[1024]{0:T(1024)}, u32[]{:S(2)}) copy-start(f32[1024]{0:T(1024)} %param.19) | copy-start | bytes 12292
  112.9 1.0 copy-start.5
  114.2 7.6 %copy-start.11 = (f32[2,64]{1,0:T(2,128)S(1)}, f32[2,64]{1,0:T(2,128)}, u32[]{:S(2)}) copy-start(f32[2,64]{1,0:T(2,128)} %param.23) | copy-start | bytes 1540
  116.3 31.7 %all-to-all-start = ((bf16[2,256,1024]{2,0,1:T(2,128)(2,1)}), bf16[2,256,1024]{2,0,1:T(2,128)(2,1)S(1)}, u32[]{:S(2)}, u32[]{:S(2)}) async-start(bf16[2,256,1024]{2,0,1:T(2,128)(2,1)} %copy.73), calls=%async_computation | async-start | bytes 2097152 | tf_op jit(solution)/shard_map/all_to_all | solution.py:87
  148.0 1.2 copy-start.14
  148.3 1.7 copy-start.7
  149.9 1.0 copy-start.4
  184.3 29.7 %copy-start.6 = (bf16[512,1024]{1,0:T(8,128)(2,1)S(1)}, bf16[512,1024]{1,0:T(8,128)(2,1)}, u32[]{:S(2)}) copy-start(bf16[512,1024]{1,0:T(8,128)(2,1)} %copy-done.5) | copy-start | bytes 3145732
  184.3 29.7 %copy-start.12 = (bf16[1024,1024]{1,0:T(8,128)(2,1)S(1)}, bf16[1024,1024]{1,0:T(8,128)(2,1)}, u32[]{:S(2)}) copy-start(bf16[1024,1024]{1,0:T(8,128)(2,1)} %param.22) | copy-start | bytes 6291460
Sparse Core Ops, SparseCore 0:
  14.4 19.5 all-gather.4
  35.5 16.8 all-gather.2
where the time goes:
time: 224 us; the launch traced here: 223 us
  matrix products  54 us (24%)
  waiting for transfers between devices  47.3 us (21%)
  local copies, waits for them, and re-layouts  46.6 us (21%)
  blocking collectives  29.6 us (13%)
  other arithmetic  26.1 us (12%)
  between operations  13.8 us (6%)
  starting transfers between devices  5.56 us (2%)
    all_to_all x1, blocking collectives, body(): lax.all_to_all(time_att, 'frames', split_axis=0, concat_axis=1, tiled=True)  29.6 us
    dot_general x3, matrix products, attend(): jnp.einsum('nkgd,mkd->kgnm', grouped, key_heads, preferred_element_type=j...  23.1 us
    all_to_all x1, waiting for transfers between devices, body(): lax.all_to_all(normed_time.reshape(frames_here, rows_here, model_width),...  22.1 us
    dot_general x3, matrix products, attend(): jnp.einsum('kgnm,mkd->nkgd', weights, value_heads, preferred_element_type...  19.9 us
    reduce_sum x3, other arithmetic, attend(): totals = jnp.sum(expos, axis=-1)  18.8 us
    all_gather x1, waiting for transfers between devices, body(): lax.all_gather(values, 'band', axis=1, tiled=True)  18.4 us
    unnamed x33, local copies, waits for them, and re-layouts  13.1 us
    convert_element_type x3, local copies, waits for them, and re-layouts, project(): queries.reshape(row_count, -1).astype(jnp.bfloat16)  7.23 us
  transfers between devices with their start and end apart: 3, of which 3 were waited for; matrix products, arithmetic and copies ran while one was open for 7% of the time, Pallas kernels for 0%

commit v1 on v0

--- a/solution.py
+++ b/solution.py
@@ -72,7 +72,7 @@
     values = values.reshape(frames_here, rows_here, -1)
     all_keys, all_values = (
         lax.all_gather(key_rows, "band", axis=1, tiled=True),
-        lax.all_gather(values, "band", axis=1, tiled=True),
+        jnp.concatenate(lax.all_gather(values, "band"), axis=1),
     )
 
     def space_frame(pieces):

time: 224 us -> 222 us (level)
  waiting for transfers between devices: 47.3 us -> 43.1 us
    all_gather x1, waiting for transfers between devices: 18.4 us -> 4.79 us  [body(): lax.all_gather(values, 'band')]
    all_gather x1, waiting for transfers between devices: 6.75 us -> 16.1 us  [body(): lax.all_gather(key_rows, 'band', axis=1, tiled=True)]
    all_gather x0 -> x1, local copies, waits for them, and re-layouts: none -> 2.29 us  [body(): lax.all_gather(values, 'band')]
    dynamic_slice x4 -> x8, local copies, waits for them, and re-layouts: 4.7 us -> 4.81 us  [body(): attended = lax.map(space_frame, (queries, all_keys, all_values))]
  transfers between devices with their start and end apart: 3 -> 3, of which waited for: 3 -> 3; matrix products, arithmetic and copies ran while one was open for 7% -> 9% of each run, Pallas kernels for 0% -> 0%
where the time goes in v1:
time: 222 us; the launch traced here: 221 us
  matrix products  54 us (24%)
  local copies, waits for them, and re-layouts  47.8 us (22%)
  waiting for transfers between devices  43.1 us (19%)
  blocking collectives  29.6 us (13%)
  other arithmetic  27.2 us (12%)
  between operations  13.8 us (6%)
  starting transfers between devices  5.56 us (3%)
    all_to_all x1, blocking collectives, body(): lax.all_to_all(time_att, 'frames', split_axis=0, concat_axis=1, tiled=True)  29.6 us
    dot_general x3, matrix products, attend(): jnp.einsum('nkgd,mkd->kgnm', grouped, key_heads, preferred_element_type=j...  23.1 us
    all_to_all x1, waiting for transfers between devices, body(): lax.all_to_all(normed_time.reshape(frames_here, rows_here, model_width),...  22.1 us
    dot_general x3, matrix products, attend(): jnp.einsum('kgnm,mkd->nkgd', weights, value_heads, preferred_element_type...  19.8 us
    reduce_sum x3, other arithmetic, attend(): totals = jnp.sum(expos, axis=-1)  18.8 us
    all_gather x1, waiting for transfers between devices, body(): lax.all_gather(key_rows, 'band', axis=1, tiled=True)  16.1 us
    unnamed x33, local copies, waits for them, and re-layouts  13.1 us
    convert_element_type x3, local copies, waits for them, and re-layouts, project(): queries.reshape(row_count, -1).astype(jnp.bfloat16)  7.23 us
  transfers between devices with their start and end apart: 3, of which 3 were waited for; matrix products, arithmetic and copies ran while one was open for 9% of the time, Pallas kernels for 0%

profile of v1, /device:TPU:0, one launch (start us, length us, event | category | flops | bytes accessed | tf_op | source)
XLA Modules:
  0.0 221.1 jit_solution(2989229626650198183)
XLA Ops:
  16.0 4.0 %copy.69 = bf16[1024,1024]{0,1:T(8,128)(2,1)} copy(bf16[1024,1024]{1,0:T(8,128)(2,1)} %param.15) | data formatting | bytes 4194304 | tf_op args[2]
  24.6 2.4 %copy.71 = bf16[2,256,1024]{1,2,0:T(8,128)(2,1)} copy(bf16[2,256,1024]{1,0,2:T(2,128)(2,1)} %convert_element_type.87) | data formatting | bytes 2097152 | tf_op jit(solution)/shard_map/while | solution.py:82
  27.0 4.8 %all-gather.3.cloned.1.call-done = bf16[4,2,256,256]{3,2,1,0:T(8,128)(2,1)} async-done(((bf16[1,2,256,256]{3,2,1,0:T(8,128)(2,1)}), bf16[4,2,256,256]{3,2,1,0:T(8,128)(2,1)}) %all-gather.3.cloned.1.call-update) | async-done | bytes 1048592 | tf_op jit(solution)/shard_map/all_gather | solution.py:75
  34.1 16.1 %all-gather.5.cloned.1.call-done = bf16[2,1024,256]{1,2,0:T(8,128)(2,1)} async-done(((bf16[2,256,256]{1,2,0:T(8,128)(2,1)}), bf16[2,1024,256]{1,2,0:T(8,128)(2,1)}) %all-gather.5.cloned.1.call-update) | async-done | bytes 1048592 | tf_op jit(solution)/shard_map/all_gather | solution.py:74
  50.2 57.8 %while.10 = (s32[]{:T(128)}, bf16[2,256,1024]{2,1,0:T(8,128)(2,1)}, bf16[2,1024,256]{2,1,0:T(8,128)(2,1)}, bf16[2,1024,256]{1,2,0:T(8,128)(2,1)}, bf16[2,256,1024]{1,2,0:T(8,128)(2,1)}, /*index=5*/s32[]{:T(128)}) while((s32[]{:T(128)}, bf16[2,256,1024]{2,1,0:T(8,128)(2,1)}, bf16[2,1024,256]{2,1,0:T(8,128)(2,1)}, ...), condition=%wide.region_6.7_spmd, body=%wide.region_3.6_spmd.sunk | while | flops 1107812352 | bytes 62997100 | solution.py:82
  52.4 8.1 %bitcast_reduce_fusion.4 = (f32[4,4,256]{2,1,0:T(4,128)S(1)}, f32[4,1024,256,4]{2,1,3,0:T(8,128)}) fusion(bf16[1024,4,64,1]{0,2,3,1:T(8,128)(2,1)S(1)} %bitcast.155, bf16[256,4,4,64]{0,3,2,1:T(8,128)(2,1)S(1)} %bitcast.156), kind=kOutput, calls=%fused_computation.1.clone.1 | convolution fusion | flops 545255424 | bytes 17842176 | tf_op jit(solution)/shard_map/while/body/eval_jaxpr/nkgd,mkd->kgnm/dot_general | solution.py:39
  60.5 8.6 %fusion.63 = f32[4,4,256]{2,1,0:T(4,128)S(1)} fusion(f32[4,1024,256,4]{2,1,3,0:T(8,128)} %get-tuple-element.112, f32[4,4,256]{2,1,0:T(4,128)S(1)} %get-tuple-element.113), kind=kLoop, calls=%fused_computation.3.clone.1 | loop fusion | flops 12578816 | bytes 16809984 | tf_op jit(solution)/shard_map/while/body/eval_jaxpr/reduce_sum | solution.py:46
  69.4 8.7 %divide_convert_fusion.2 = bf16[256,4,4,64]{0,3,2,1:T(8,128)(2,1)S(1)} fusion(bf16[1024,4,64,1]{0,2,3,1:T(8,128)(2,1)S(1)} %bitcast.153, f32[4,1024,256,4]{2,1,3,0:T(8,128)} %get-tuple-element.112, f32[4,4,256]{2,1,0:T(4,128)S(1)} %get-tuple-element.113, f32[256,4,4]{0,2,1:T(4,128)S(1)} %bitcast.163), kind=kOutput, calls=%fused_computation.7.clone.1 | convolution fusion | flops 549978112 | bytes 17858560 | tf_op jit(solution)/shard_map/while/body/eval_jaxpr/kgnm,mkd->nkgd/dot_general | solution.py:48
  81.3 8.1 %bitcast_reduce_fusion.4 = (f32[4,4,256]{2,1,0:T(4,128)S(1)}, f32[4,1024,256,4]{2,1,3,0:T(8,128)}) fusion(bf16[1024,4,64,1]{0,2,3,1:T(8,128)(2,1)S(1)} %bitcast.155, bf16[256,4,4,64]{0,3,2,1:T(8,128)(2,1)S(1)} %bitcast.156), kind=kOutput, calls=%fused_computation.1.clone.1 | convolution fusion | flops 545255424 | bytes 17842176 | tf_op jit(solution)/shard_map/while/body/eval_jaxpr/nkgd,mkd->kgnm/dot_general | solution.py:39
  89.4 8.6 %fusion.63 = f32[4,4,256]{2,1,0:T(4,128)S(1)} fusion(f32[4,1024,256,4]{2,1,3,0:T(8,128)} %get-tuple-element.112, f32[4,4,256]{2,1,0:T(4,128)S(1)} %get-tuple-element.113), kind=kLoop, calls=%fused_computation.3.clone.1 | loop fusion | flops 12578816 | bytes 16809984 | tf_op jit(solution)/shard_map/while/body/eval_jaxpr/reduce_sum | solution.py:46
  98.2 8.7 %divide_convert_fusion.2 = bf16[256,4,4,64]{0,3,2,1:T(8,128)(2,1)S(1)} fusion(bf16[1024,4,64,1]{0,2,3,1:T(8,128)(2,1)S(1)} %bitcast.153, f32[4,1024,256,4]{2,1,3,0:T(8,128)} %get-tuple-element.112, f32[4,4,256]{2,1,0:T(4,128)S(1)} %get-tuple-element.113, f32[256,4,4]{0,2,1:T(4,128)S(1)} %bitcast.163), kind=kOutput, calls=%fused_computation.7.clone.1 | convolution fusion | flops 549978112 | bytes 17858560 | tf_op jit(solution)/shard_map/while/body/eval_jaxpr/kgnm,mkd->nkgd/dot_general | solution.py:48
  108.0 2.9 %fusion.15 = (f32[512]{0:T(512)S(1)}, bf16[512,1024]{1,0:T(8,128)(2,1)S(1)}) fusion(bf16[512,1024]{1,0:T(8,128)(2,1)} %bitcast.182, bf16[1024,1024]{1,0:T(8,128)(2,1)S(1)} %copy-done, bf16[2,256,1024]{2,1,0:T(8,128)(2,1)} %param.13), kind=kOutput, calls=%fused_computation.23 | convolution fusion | flops 1076887040 | bytes 5244928 | tf_op jit(solution)/shard_map/dot_general | solution.py:84
  114.3 5.5 %all-to-all-start = ((bf16[2,256,1024]{2,0,1:T(2,128)(2,1)}), bf16[2,256,1024]{2,0,1:T(2,128)(2,1)S(1)}, u32[]{:S(2)}, u32[]{:S(2)}) async-start(bf16[2,256,1024]{2,0,1:T(2,128)(2,1)} %copy.73), calls=%async_computation | async-start | bytes 2097152 | tf_op jit(solution)/shard_map/all_to_all | solution.py:87
  119.9 3.9 %copy.79 = bf16[1024,1024]{0,1:T(8,128)(2,1)} copy(bf16[1024,1024]{1,0:T(8,128)(2,1)} %param.20) | data formatting | bytes 4194304 | tf_op args[7]
  123.9 22.1 %all-to-all-done = bf16[2,256,1024]{2,0,1:T(2,128)(2,1)S(1)} async-done(((bf16[2,256,1024]{2,0,1:T(2,128)(2,1)}), bf16[2,256,1024]{2,0,1:T(2,128)(2,1)S(1)}, u32[]{:S(2)}, u32[]{:S(2)}) %all-to-all-start) | async-done | bytes 1048608 | tf_op jit(solution)/shard_map/all_to_all | solution.py:87
  151.8 3.2 %multiply_reduce_fusion = (f32[512,16]{0,1:T(8,128)S(1)}, f32[512,16,64]{0,2,1:T(8,128)S(1)}) fusion(bf16[512,1024,1]{1,0,2:T(8,128)(2,1)} %bitcast.173, bf16[16,64,1024]{2,1,0:T(8,128)(2,1)} %bitcast.164), kind=kOutput, calls=%fused_computation.43 | convolution fusion | flops 1074782208 | bytes 5275648 | tf_op jit(solution)/shard_map/dot_general | solution.py:19
  155.5 2.9 %copy.80 = bf16[512,16,64]{2,1,0:T(8,128)(2,1)} copy(bf16[512,16,64]{0,2,1:T(8,128)(2,1)S(1)} %multiply_convert_fusion) | data formatting | bytes 2097152 | tf_op jit(solution)/shard_map/convert_element_type | solution.py:26
  158.4 3.2 %convert_element_type.93 = bf16[16,32,1024]{2,1,0:T(8,128)(2,1)S(1)} reshape(bf16[512,16,64]{2,1,0:T(8,128)(2,1)} %copy.80) | data formatting | bytes 2097152 | tf_op jit(solution)/shard_map/convert_element_type | solution.py:26
  161.7 2.4 %reshape.190 = bf16[32,16,4,4,64]{4,3,2,0,1:T(4,128)(2,1)} reshape(bf16[32,16,1024]{2,0,1:T(8,128)(2,1)S(1)} %bitcast.158) | data formatting | bytes 2097152 | tf_op jit(solution)/shard_map/vmap()/reshape | solution.py:36
  164.4 6.9 %fusion.14 = (f32[32,4,4,16]{3,2,1,0:T(4,128)S(1)}, f32[32,4,16,16,4]{3,2,4,1,0:T(8,128)S(1)}) fusion(pred[16,16]{0,1:T(8,128)(4,1)S(1)} %iota_compare_fusion, bf16[32,16,4,4,64]{4,3,2,0,1:T(4,128)(2,1)} %reshape.190, bf16[32,16,4,64,1]{3,2,1,0,4:T(4,128)(2,1)} %bitcast.168), kind=kOutput, calls=%fused_computation.19 | convolution fusion | flops 17162240 | bytes 1868032 | tf_op jit(solution)/shard_map/vmap(nkgd,mkd->kgnm)/dot_general | solution.py:39
  172.9 2.4 %fusion.11 = bf16[32,16,4,4,64]{4,1,3,2,0:T(8,128)(2,1)S(1)} fusion(f32[32,4,16,16,4]{3,2,4,1,0:T(8,128)S(1)} %get-tuple-element.78, f32[32,16,4,4]{1,3,2,0:T(4,128)S(1)} %bitcast.180, f32[32,4,4,16]{3,2,1,0:T(4,128)S(1)} %get-tuple-element.77, pred[16,16]{0,1:T(8,128)(4,1)S(1)} %iota_compare_fusion, bf16[32,16,4,64,1]{3,2,1,0,4:T(4,128)(2,1)S(1)} %bitcast.179), kind=kOutput, calls=%fused_computation.14 | convolution fusion | flops 18350080 | bytes 1900800 | tf_op jit(solution)/shard_map/vmap(kgnm,mkd->nkgd)/dot_general | solution.py:48
  175.4 2.5 %copy.86 = bf16[32,16,4,4,64]{4,3,2,1,0:T(4,128)(2,1)} copy(bf16[32,16,4,4,64]{4,1,3,2,0:T(8,128)(2,1)S(1)} %fusion.11) | data formatting | bytes 2097152 | tf_op jit(solution)/shard_map/vmap()/convert_element_type | solution.py:50
  177.8 3.8 %convert_element_type.96 = bf16[32,16,1024]{2,1,0:T(8,128)(2,1)S(1)} reshape(bf16[32,16,4,4,64]{4,3,2,1,0:T(4,128)(2,1)} %copy.86) | data formatting | bytes 2097152 | tf_op jit(solution)/shard_map/vmap()/convert_element_type | solution.py:50
  182.3 29.6 %all_to_all.30 = bf16[16,32,1024]{2,1,0:T(8,128)(2,1)S(1)} all-to-all(bf16[16,32,1024]{2,1,0:T(8,128)(2,1)S(1)} %copy.87), channel_id=1, replica_groups=mesh['frames'=8,'band'=4] {'frames'}, dimensions={0} | all-to-all | bytes 2097152 | tf_op jit(solution)/shard_map/all_to_all | solution.py:107
  (101 shorter events, 37.7 us)
Async XLA Ops:
  6.5 101.4 %copy-start = (bf16[1024,1024]{1,0:T(8,128)(2,1)S(1)}, bf16[1024,1024]{1,0:T(8,128)(2,1)}, u32[]{:S(2)}) copy-start(bf16[1024,1024]{1,0:T(8,128)(2,1)} %param.17) | copy-start | bytes 6291460
  6.5 3.2 %copy-start.14 = (bf16[1024,512]{1,0:T(8,128)(2,1)S(1)}, bf16[1024,512]{1,0:T(8,128)(2,1)}, u32[]{:S(2)}) copy-start(bf16[1024,512]{1,0:T(8,128)(2,1)} %param.16) | copy-start | bytes 3145732
  6.5 25.3 %all-gather.3.cloned.1.call-start = ((), (), s32[]{:S(2)}) async-start(), calls=%async_computation.2 | async-start | bytes 1310720 | tf_op jit(solution)/shard_map/all_gather | solution.py:75
  10.5 1.0 copy-start.4
  12.2 1.7 copy-start.11
  12.2 38.0 %all-gather.5.cloned.1.call-start = ((), (), s32[]{:S(2)}) async-start(), calls=%async_computation.3 | async-start | bytes 1310720 | tf_op jit(solution)/shard_map/all_gather | solution.py:74
  16.0 4.0 %copy-start.2 = (bf16[2,256,1024]{2,1,0:T(8,128)(2,1)S(1)}, bf16[2,256,1024]{2,1,0:T(8,128)(2,1)}, u32[]{:S(2)}) copy-start(bf16[2,256,1024]{2,1,0:T(8,128)(2,1)} %param.13) | copy-start | bytes 3145732
  16.0 4.0 %copy-start.9 = (f32[1024]{0:T(1024)S(1)}, f32[1024]{0:T(1024)}, u32[]{:S(2)}) copy-start(f32[1024]{0:T(1024)} %param.14) | copy-start | bytes 12292
  20.0 1.7 copy-start.3
  60.5 8.6 %copy-start.1 = (bf16[2,1024,256]{2,1,0:T(8,128)(2,1)S(1)}, bf16[2,1024,256]{2,1,0:T(8,128)(2,1)}, u32[]{:S(2)}) copy-start(bf16[2,1024,256]{2,1,0:T(8,128)(2,1)} %get-tuple-element.128) | copy-start | bytes 3145732 | tf_op jit(solution)/shard_map/while
  89.4 8.6 %copy-start.1 = (bf16[2,1024,256]{2,1,0:T(8,128)(2,1)S(1)}, bf16[2,1024,256]{2,1,0:T(8,128)(2,1)}, u32[]{:S(2)}) copy-start(bf16[2,1024,256]{2,1,0:T(8,128)(2,1)} %get-tuple-element.128) | copy-start | bytes 3145732 | tf_op jit(solution)/shard_map/while
  108.0 3.9 %copy-start.10 = (f32[1024]{0:T(1024)S(1)}, f32[1024]{0:T(1024)}, u32[]{:S(2)}) copy-start(f32[1024]{0:T(1024)} %param.19) | copy-start | bytes 12292
  110.9 1.0 copy-start.6
  112.2 7.6 %copy-start.12 = (f32[2,64]{1,0:T(2,128)S(1)}, f32[2,64]{1,0:T(2,128)}, u32[]{:S(2)}) copy-start(f32[2,64]{1,0:T(2,128)} %param.23) | copy-start | bytes 1540
  114.3 31.7 %all-to-all-start = ((bf16[2,256,1024]{2,0,1:T(2,128)(2,1)}), bf16[2,256,1024]{2,0,1:T(2,128)(2,1)S(1)}, u32[]{:S(2)}, u32[]{:S(2)}) async-start(bf16[2,256,1024]{2,0,1:T(2,128)(2,1)} %copy.73), calls=%async_computation | async-start | bytes 2097152 | tf_op jit(solution)/shard_map/all_to_all | solution.py:87
  146.0 1.2 copy-start.15
  146.3 1.7 copy-start.8
  147.9 1.0 copy-start.5
  182.3 29.7 %copy-start.7 = (bf16[512,1024]{1,0:T(8,128)(2,1)S(1)}, bf16[512,1024]{1,0:T(8,128)(2,1)}, u32[]{:S(2)}) copy-start(bf16[512,1024]{1,0:T(8,128)(2,1)} %copy-done.6) | copy-start | bytes 3145732
  182.3 29.7 %copy-start.13 = (bf16[1024,1024]{1,0:T(8,128)(2,1)S(1)}, bf16[1024,1024]{1,0:T(8,128)(2,1)}, u32[]{:S(2)}) copy-start(bf16[1024,1024]{1,0:T(8,128)(2,1)} %param.22) | copy-start | bytes 6291460
Sparse Core Ops, SparseCore 0:
  12.3 19.4 all-gather.2
  33.4 16.8 all-gather.4
